TPU v7x, 32 devices: a whole 2x2x4 slice. The times are simulated.
32 devices in a mesh: grp: 2 (over x), wide: 16 (over z, y, core).
Axes of the slice: x: 2, y: 2, z: 4, core: 2. Of those that a mesh axis runs over, the one named last changes fastest.
Arguments:
- voltages: bfloat16 [2048, 2, 8240], P(('grp', 'wide')), parts along dimension 0, may hold values from -6 to 6
- taps: float32 [4, 16], replicated, may hold values from -3 to 3
- flags: int32 [2048], P(('grp', 'wide')), parts along dimension 0, may hold values 0 or 1
- positions: float32 [2, 1024], replicated, may hold values from -20 to 20
- beam_index: int32 [512], P('grp'), parts along dimension 0, may hold values from 0 to 1023
Outputs:
- power: float32 [512, 16, 128], P(('grp', 'wide')), parts along dimension 0
There are 2 independent parts, one for each index of `grp`. A program takes and returns all parts, laid end to end along the dimension named above; an argument that names none is the same for every part. Nothing has to cross between parts.
Inputs may be any that keep to these rules, and one draw needn't show every extreme that they name: 1 keeps an antenna, 0 flags it.
All inputs are finite; a program needn't handle non-finite values. No bound on the sum of `flags` on one device may be relied on, other than what follows from the above.
Results may differ from a plain program's by a relative error of at most 0.0075.
Values may be sent and summed in bfloat16 or wider, within the bound.
No kernel may reach another device: no remote copies, remote signals or barrier semaphores. Data moves between devices by JAX's collectives and lax.ppermute only.
A program may use at most 128 MiB of HBM per device.

v0:
```python
import functools
import math

import jax
import jax.numpy as jnp
import numpy as np
from jax import lax
from jax.experimental import pallas as pl
from jax.experimental.pallas import tpu as pltpu
from jax.sharding import PartitionSpec as P

ITERS = 2

damping = 0.5
grid_side = 32
group = 4
LANES = 128
PACK = 16

NT = (((1,), (1,)), ((), ()))
NN = (((1,), (0,)), ((), ()))


def round_up(value, unit):
    return -(-value // unit) * unit


def dot(a, b, dims):
    return lax.dot_general(a, b, dims, preferred_element_type=jnp.float32)


def swap_pairs(x):
    lane = lax.broadcasted_iota(jnp.int32, x.shape, x.ndim - 1)
    width = x.shape[-1]
    after = pltpu.roll(x, width - 1, x.ndim - 1)
    before = pltpu.roll(x, 1, x.ndim - 1)
    return jnp.where(lane % 2 == 0, -after, before)


class Plan:
    def __init__(self, count, length, ntaps, chans):
        self.rows = 2 * count
        self.count = count
        self.chans = chans
        self.ntaps = ntaps
        self.total = length // chans - ntaps + 1
        self.block = max(LANES, chans)
        self.per = self.block // chans
        self.reach = self.block + (ntaps - 1) * chans
        self.window = round_up(self.reach, LANES)
        self.length = length
        self.step = PACK // self.per
        self.steps = self.total // PACK


def dft_tables(plan):
    row = np.arange(plan.chans * plan.per)
    chan = row // plan.per
    lane = np.arange(plan.window)
    angle = 2.0 * np.pi / plan.chans * ((chan[:, None] * (lane % plan.chans)[None, :]) % plan.chans)
    return np.cos(angle).astype(np.float32), np.sin(angle).astype(np.float32)


def channelize_kernel(plan, taps_ref, keep_ref, cos_ref, sin_ref, v_ref, o_ref, w_ref):
    n = plan.chans * plan.per
    row = lax.broadcasted_iota(jnp.int32, (n, plan.window), 0)
    lane = lax.broadcasted_iota(jnp.int32, (n, plan.window), 1)
    behind = lane // plan.chans - row % plan.per
    coef = jnp.zeros((n, plan.window), jnp.float32)
    for tap in range(plan.ntaps):
        coef = jnp.where(behind == tap, taps_ref[tap : tap + 1, :], coef)
    for part, table in enumerate((cos_ref, sin_ref)):
        full = coef * table[...]
        high = full.astype(jnp.bfloat16)
        w_ref[part * n : (part + 1) * n] = high
        w_ref[(2 + part) * n : (3 + part) * n] = (full - high.astype(jnp.float32)).astype(jnp.bfloat16)
    keep = jnp.concatenate([keep_ref[...]] * plan.step, axis=1)

    def emit(step, pieces):
        x = pieces[0] if len(pieces) == 1 else jnp.concatenate(pieces, axis=0)
        width = x.shape[1]
        d = dot(w_ref[:, :width], x, NT)
        d = d[: 2 * n] + d[2 * n :]
        out = (d[:n] - swap_pairs(d[n:])) * keep
        if plan.per * plan.step == PACK and plan.per == 8 and plan.rows == LANES:
            for chan in range(plan.chans):
                part = out[chan * plan.per : (chan + 1) * plan.per]
                both = jnp.concatenate([part[:, :LANES], part[:, LANES:]], axis=0)
                o_ref[chan, pl.ds(pl.multiple_of(step * PACK, PACK), PACK), :] = both.astype(jnp.bfloat16)
        else:
            o_ref[pl.ds(step, 1)] = out.astype(jnp.bfloat16)[None]

    def load(start, width):
        return v_ref[:, :, pl.ds(start, width)].reshape(plan.rows, width)

    def body(step, carry):
        base = pl.multiple_of(step * plan.step * plan.block, LANES)
        emit(step, [load(pl.multiple_of(base + i * plan.block, LANES), plan.window) for i in range(plan.step)])
        return carry

    lax.fori_loop(0, plan.steps - 1, body, 0)
    step = plan.steps - 1
    pieces = []
    for i in range(plan.step):
        start = (step * plan.step + i) * plan.block
        width = min(plan.window, plan.length - start)
        piece = load(start, width)
        if width < plan.window:
            fill = jnp.zeros((plan.rows, plan.window - width), piece.dtype)
            piece = jnp.concatenate([piece, fill], axis=1)
        pieces.append(piece)
    emit(step, pieces)


def channelize(voltages, taps, flags):
    count, _, length = voltages.shape
    ntaps, chans = taps.shape
    plan = Plan(count, length, ntaps, chans)
    keep = jnp.repeat(flags.astype(jnp.float32) / math.sqrt(chans), 2)[None, :]
    wide_taps = jnp.tile(taps, (1, plan.window // chans))
    cosine, sine = dft_tables(plan)
    direct = plan.per == 8 and plan.step == 2 and plan.rows == LANES
    n = plan.chans * plan.per
    if direct:
        shape = (chans, plan.total, plan.rows)
    else:
        shape = (plan.steps, n, plan.step * plan.rows)
    out = pl.pallas_call(
        functools.partial(channelize_kernel, plan),
        out_shape=jax.ShapeDtypeStruct(shape, jnp.bfloat16),
        scratch_shapes=[pltpu.VMEM((4 * n, plan.window), jnp.bfloat16)],
        name="channelize",
    )(wide_taps, keep, jnp.asarray(cosine), jnp.asarray(sine), voltages)
    if not direct:
        out = out.reshape(plan.steps, chans, plan.per, plan.step, plan.rows)
        out = out.transpose(1, 0, 3, 2, 4).reshape(chans, plan.total, plan.rows)
    return out


def steer_kernel(scale_ref, positions_ref, index_ref, o_ref):
    beams = index_ref.shape[1]
    row = lax.broadcasted_iota(jnp.int32, (beams, beams), 0)
    lane = lax.broadcasted_iota(jnp.int32, (beams, beams), 1)

    def column(line):
        return jnp.sum(jnp.where(row == lane, line, 0.0), axis=1, keepdims=True)

    index = index_ref[...]
    east = column((index % grid_side).astype(jnp.float32))
    north = column((index // grid_side).astype(jnp.float32))
    east = (east + 0.5) / grid_side - 0.5
    north = (north + 0.5) / grid_side - 0.5
    ratio = scale_ref[...]
    width = 2 * LANES

    def body(i, carry):
        where = pl.ds(pl.multiple_of(i * width, width), width)
        turns = ratio * (positions_ref[0:1, where] * east + positions_ref[1:2, where] * north)
        turns = turns - jnp.round(turns)
        odd = lax.broadcasted_iota(jnp.int32, turns.shape, 1) % 2
        turns = jnp.where(odd == 1, turns + 0.25, turns)
        turns = turns - jnp.round(turns)
        o_ref[:, where] = cos_turns(turns)
        return carry

    lax.fori_loop(0, positions_ref.shape[1] // width, body, 0)


def cos_turns(t):
    u = 0.25 - jnp.abs(t)
    s = u * u
    acc = jnp.full_like(s, SINE[-1])
    for c in SINE[-2::-1]:
        acc = acc * s + c
    return acc * u


SINE = [(-1) ** k * (2.0 * math.pi) ** (2 * k + 1) / math.factorial(2 * k + 1) for k in range(8)]


def steering(channel, positions, beam_index, chans):
    count = positions.shape[1]
    beams = beam_index.shape[0]
    ratio = (1.0 + 0.5 * channel.astype(jnp.float32) / chans).reshape(1, 1)
    return pl.pallas_call(
        steer_kernel,
        out_shape=jax.ShapeDtypeStruct((beams, 2 * count), jnp.float32),
        cost_estimate=pl.CostEstimate(flops=60 * beams * count, bytes_accessed=8 * beams * count, transcendentals=0),
        name="steer",
    )(ratio, jnp.repeat(positions, 2, axis=1), beam_index[None, :])


def solve_kernel(steer_ref, x_ref, o_ref, xx_ref, w_ref, low_ref, u_ref):
    sources, total, width = x_ref.shape
    lanes = sources * width
    count = lanes // 2
    beams = steer_ref.shape[0]

    squares = []
    for src in range(sources):
        where = slice(src * width, (src + 1) * width)

        def body(i, acc):
            at = pl.ds(pl.multiple_of(i * 64, 64), 64)
            x = x_ref[src, at, :]
            f = x.astype(jnp.float32)
            xx_ref[at, where] = x
            xx_ref[pl.ds(pl.multiple_of(total + i * 64, 64), 64), where] = swap_pairs(f).astype(jnp.bfloat16)
            return acc + jnp.sum((f * f).reshape(8, 8, width), axis=0)

        acc = lax.fori_loop(0, total // 64, body, jnp.zeros((8, width), jnp.float32))
        squares.append(jnp.sum(acc, axis=0, keepdims=True))
    square = jnp.concatenate(squares, axis=1)
    lane = lax.broadcasted_iota(jnp.int32, square.shape, 1)
    other = jnp.where(lane % 2 == 0, pltpu.roll(square, lanes - 1, 1), pltpu.roll(square, 1, 1))
    diagonal = (square + other) / total
    loading = jnp.sum(square, axis=1, keepdims=True) / (total * count) + 1e-05
    scaling = damping / (diagonal + loading)

    w = scaling * steer_ref[...]
    w_ref[...] = w
    low_ref[...] = w.astype(jnp.bfloat16)
    tile = 512

    def project():
        def body(i, carry):
            at = pl.ds(pl.multiple_of(i * tile, tile), tile)
            u_ref[:, at] = dot(low_ref[...], xx_ref[at, :], NT)
            return carry

        lax.fori_loop(0, 2 * total // tile, body, 0)

    for _ in range(ITERS):
        project()
        u_low = (u_ref[...] / total).astype(jnp.bfloat16)
        for i in range(lanes // tile):
            at = slice(i * tile, (i + 1) * tile)
            image = dot(u_low, xx_ref[:, at], NN)
            w = w_ref[:, at]
            w = w + scaling[:, at] * (steer_ref[:, at] - (image + loading * w))
            w_ref[:, at] = w
            low_ref[:, at] = w.astype(jnp.bfloat16)
    project()

    beam = (u_ref[...] * (1.0 / math.sqrt(count))).astype(jnp.bfloat16).astype(jnp.float32)
    square = beam * beam
    energy = square[:, :total] + square[:, total:]
    high = energy.astype(jnp.bfloat16)
    rest = (energy - high.astype(jnp.float32)).astype(jnp.bfloat16)
    row = lax.broadcasted_iota(jnp.int32, (total, total // group), 0)
    lane = lax.broadcasted_iota(jnp.int32, (total, total // group), 1)
    pick = jnp.where(row // group == lane, 1.0, 0.0).astype(jnp.bfloat16)
    o_ref[...] = (dot(high, pick, NN) + dot(rest, pick, NN)).astype(jnp.bfloat16)


def solve(steer, x):
    beams, lanes = steer.shape
    total = x.shape[1]
    return pl.pallas_call(
        solve_kernel,
        out_shape=jax.ShapeDtypeStruct((beams, total // group), jnp.bfloat16),
        scratch_shapes=[
            pltpu.VMEM((2 * total, lanes), jnp.bfloat16),
            pltpu.VMEM((beams, lanes), jnp.float32),
            pltpu.VMEM((beams, lanes), jnp.bfloat16),
            pltpu.VMEM((beams, 2 * total), jnp.float32),
        ],
        compiler_params=pltpu.CompilerParams(vmem_limit_bytes=40 * 2**20),
        name="solve",
    )(steer, x)


def local(voltages, taps, flags, positions, beam_index):
    chans = taps.shape[1]
    peers = lax.axis_size("wide")
    per_dev = chans // peers
    first = lax.axis_index("wide") * per_dev
    spectra = channelize(voltages, taps, flags)
    rows = spectra.shape[2]
    total = spectra.shape[1]
    moved = lax.all_to_all(spectra, "wide", split_axis=0, concat_axis=0, tiled=True)
    moved = moved.reshape(peers, per_dev, total, rows)
    spectra, positions, beam_index = lax.optimization_barrier((spectra, positions, beam_index))
    powers = []
    for offset in range(per_dev):
        steer = steering(first + offset, positions, beam_index, chans)
        x = moved[:, offset]
        if rows % LANES:
            x = x.transpose(1, 0, 2).reshape(1, total, peers * rows)
        powers.append(solve(steer, x))
    power = jnp.stack(powers)
    result = lax.all_to_all(power, "wide", split_axis=1, concat_axis=0, tiled=True)
    return jnp.transpose(result.astype(jnp.float32), (1, 0, 2))


def solution(mesh):
    in_specs = (P(("grp", "wide"), None, None), P(), P(("grp", "wide")), P(), P("grp"))
    out_specs = P(("grp", "wide"), None, None)
    return jax.shard_map(local, mesh=mesh, in_specs=in_specs, out_specs=out_specs, check_vma=False)
```

profile of v0, /device:TPU:0, one launch (start us, length us, event | category | flops | bytes accessed | tf_op | source)
XLA Modules:
  0.0 107.2 jit_solution(156198650385761787)
XLA Ops:
  0.0 0.7 convert_multiply_fusion
  0.7 0.1 broadcast_in_dim.9
  0.7 0.7 broadcast_in_dim_reshape.3.keep_ref
  1.4 0.7 tile.4
  2.1 0.7 tile.10.taps_ref
  2.8 15.3 %channelize.1 = bf16[16,512,128]{2,1,0:T(8,128)(2,1)} custom-call(f32[4,256]{1,0:T(4,128)} %tile.10.taps_ref, f32[1,128]{1,0:T(1,128)} %broadcast_in_dim_reshape.3.keep_ref, f32[128,256]{1,0:T(8,128)} %constant.18.clone.cos_ref, f32[128,256]{1,0:T(8,128)} %constant.19.clone.sin_ref, bf16[64,2,8240]{2,1,0:T(2,128)(2,1)} %v_ref.1), custom_call_target="tpu_custom_call" | custom-call | tf_op jit(solution)/shard_map/channelize/pallas_call | solution.py:128
  18.1 0.0 copy-start.1
  18.1 7.5 %all-to-all-start = ((bf16[16,512,128]{2,1,0:T(8,128)(2,1)}), bf16[16,512,128]{2,1,0:T(8,128)(2,1)S(1)}, u32[]{:S(2)}, u32[]{:S(2)}) async-start(bf16[16,512,128]{2,1,0:T(8,128)(2,1)} %channelize.1), calls=%async_computation | async-start | bytes 4194304 | tf_op jit(solution)/shard_map/all_to_all | solution.py:281
  25.6 0.0 copy-done.1
  25.6 0.3 broadcast_in_dim.10
  26.0 1.2 %reshape.16.positions_ref = f32[2,2048]{1,0:T(2,128)} reshape(f32[2,1024,2]{2,1,0:T(8,128)S(1)} %broadcast_in_dim.10) | data formatting | bytes 32768 | tf_op jit(solution)/shard_map/reshape | solution.py:190
  27.2 5.2 %steer.1.steer_ref = f32[256,2048]{1,0:T(8,128)} custom-call(f32[1,1]{1,0:T(1,128)} %bitcast.scale_ref, f32[2,2048]{1,0:T(2,128)} %reshape.16.positions_ref, s32[1,256]{1,0:T(1,128)} %bitcast.15), custom_call_target="tpu_custom_call" | custom-call | flops 15728640 | bytes 2097152 | tf_op jit(solution)/shard_map/steer/pallas_call | solution.py:185
  32.4 34.2 %all-to-all-done.x_ref = bf16[16,512,128]{2,1,0:T(8,128)(2,1)S(1)} async-done(((bf16[16,512,128]{2,1,0:T(8,128)(2,1)}), bf16[16,512,128]{2,1,0:T(8,128)(2,1)S(1)}, u32[]{:S(2)}, u32[]{:S(2)}) %all-to-all-start) | async-done | bytes 2097184 | tf_op jit(solution)/shard_map/all_to_all | solution.py:281
  66.6 0.0 copy-start
  66.6 1.6 %copy-done = f32[256,2048]{1,0:T(8,128)S(1)} copy-done((f32[256,2048]{1,0:T(8,128)S(1)}, f32[256,2048]{1,0:T(8,128)}, u32[]{:S(2)}) %copy-start) | copy-done | bytes 2097176
  68.2 18.5 %solve.1 = bf16[256,128]{1,0:T(8,128)(2,1)S(1)} custom-call(f32[256,2048]{1,0:T(8,128)S(1)} %copy-done, bf16[16,512,128]{2,1,0:T(8,128)(2,1)S(1)} %all-to-all-done.x_ref), custom_call_target="tpu_custom_call" | custom-call | tf_op jit(solution)/shard_map/solve/pallas_call | solution.py:259
  86.7 0.1 copy.15
  86.8 0.5 broadcast.4
  87.3 1.0 reduce
  88.4 17.9 %all_to_all.14 = bf16[16,2,1024]{2,1,0:T(2,128)(2,1)S(1)} all-to-all(bf16[16,2,1024]{2,1,0:T(2,128)(2,1)S(1)} %reshape.18), channel_id=1, replica_groups=mesh['grp'=2,'wide'=16] {'wide'}, dimensions={0} | all-to-all | bytes 131072 | tf_op jit(solution)/shard_map/all_to_all | solution.py:292
  106.3 0.1 reshape.19
  106.3 0.1 bitcast_convert_fusion
  106.5 0.7 copy.14
  (1 shorter events, 0.0 us)
Async XLA Ops:
  18.1 7.6 %copy-start.1 = (f32[2,1024]{1,0:T(2,128)S(1)}, f32[2,1024]{1,0:T(2,128)}, u32[]{:S(2)}) copy-start(f32[2,1024]{1,0:T(2,128)} %param.10) | copy-start | bytes 24580
  18.1 48.5 %all-to-all-start = ((bf16[16,512,128]{2,1,0:T(8,128)(2,1)}), bf16[16,512,128]{2,1,0:T(8,128)(2,1)S(1)}, u32[]{:S(2)}, u32[]{:S(2)}) async-start(bf16[16,512,128]{2,1,0:T(8,128)(2,1)} %channelize.1), calls=%async_computation | async-start | bytes 4194304 | tf_op jit(solution)/shard_map/all_to_all | solution.py:281
  66.6 1.6 %copy-start = (f32[256,2048]{1,0:T(8,128)S(1)}, f32[256,2048]{1,0:T(8,128)}, u32[]{:S(2)}) copy-start(f32[256,2048]{1,0:T(8,128)} %steer.1.steer_ref) | copy-start | bytes 6291460
where the time goes:
time: 108 us; the launch traced here: 107 us
  Pallas kernels  39 us (36%)
  waiting for transfers between devices  34.2 us (32%)
  blocking collectives  17.9 us (17%)
  starting transfers between devices  7.55 us (7%)
  local copies, waits for them, and re-layouts  6.62 us (6%)
  other arithmetic  1.8 us (2%)
    all_to_all x1, waiting for transfers between devices, local(): lax.all_to_all(spectra, 'wide', split_axis=0, concat_axis=0, tiled=True)  34.2 us
    pallas_call x1, Pallas kernels, solve(): pl.pallas_call(solve_kernel, out_shape=jax.ShapeDtypeStruct((beams, total...  18.5 us
    all_to_all x1, blocking collectives, local(): lax.all_to_all(power, 'wide', split_axis=1, concat_axis=0, tiled=True)  17.9 us
    pallas_call x1, Pallas kernels, channelize(): pl.pallas_call(functools.partial(channelize_kernel, plan), out_shape=jax....  15.3 us
    all_to_all x1, starting transfers between devices, local(): lax.all_to_all(spectra, 'wide', split_axis=0, concat_axis=0, tiled=True)  7.55 us
    pallas_call x1, Pallas kernels, steering(): pl.pallas_call(steer_kernel, out_shape=jax.ShapeDtypeStruct((beams, 2 * c...  5.19 us
    unnamed x7, local copies, waits for them, and re-layouts  2.18 us
  transfers between devices with their start and end apart: 1, of which 1 were waited for; matrix products, arithmetic and copies ran while one was open for 1% of the time, Pallas kernels for 5%

commit v1 on v0

v1 whole, which is shorter than its diff:
```python
import functools
import math

import jax
import jax.numpy as jnp
import numpy as np
from jax import lax
from jax.experimental import pallas as pl
from jax.experimental.pallas import tpu as pltpu
from jax.sharding import PartitionSpec as P

ITERS = 2

damping = 0.5
grid_side = 32
group = 4
LANES = 128
PACK = 16
PART = 128
CHUNKS = (1,)

NT = (((1,), (1,)), ((), ()))
NN = (((1,), (0,)), ((), ()))


def round_up(value, unit):
    return -(-value // unit) * unit


def dot(a, b, dims):
    return lax.dot_general(a, b, dims, preferred_element_type=jnp.float32)


def swap_pairs(x):
    lane = lax.broadcasted_iota(jnp.int32, x.shape, x.ndim - 1)
    width = x.shape[-1]
    after = pltpu.roll(x, width - 1, x.ndim - 1)
    before = pltpu.roll(x, 1, x.ndim - 1)
    return jnp.where(lane % 2 == 0, -after, before)


class Plan:
    def __init__(self, count, length, ntaps, chans):
        self.count = count
        self.rows = 2 * count
        self.chans = chans
        self.ntaps = ntaps
        self.total = length // chans - ntaps + 1
        self.block = max(LANES, chans)
        self.per = self.block // chans
        self.behind = (ntaps - 1) * chans
        self.window = round_up(self.block + self.behind, LANES)
        self.step = PACK // self.per
        self.part = math.gcd(self.total, PART)
        self.samples = self.part * chans
        self.next = min(
            width
            for width in range(LANES, self.samples + 1, LANES)
            if width >= self.behind and self.samples % width == 0
        )
        self.n = self.chans * self.per
        self.direct = self.per == 8 and self.rows == LANES


def filter_matrix(plan, taps_ref, w_ref):
    n = plan.n
    lane = lax.broadcasted_iota(jnp.int32, (8, plan.window), 1) % plan.chans
    tap_rows = []
    for tap in range(plan.ntaps):
        line = jnp.zeros((8, plan.window), jnp.float32)
        for branch in range(plan.chans):
            line = jnp.where(lane == branch, taps_ref[tap, branch], line)
        tap_rows.append(line[:1])
    row = lax.broadcasted_iota(jnp.int32, (n, plan.window), 0)
    lane = lax.broadcasted_iota(jnp.int32, (n, plan.window), 1)
    behind = lane // plan.chans - row % plan.per
    coef = jnp.zeros((n, plan.window), jnp.float32)
    for tap in range(plan.ntaps):
        coef = jnp.where(behind == tap, tap_rows[tap], coef)
    cycle = ((row // plan.per) * (lane % plan.chans)) % plan.chans
    turns = cycle.astype(jnp.float32) / plan.chans
    turns = turns - jnp.round(turns)
    for part, table in enumerate((cos_turns(turns), sin_turns(turns))):
        full = coef * table
        high = full.astype(jnp.bfloat16)
        w_ref[part * n : (part + 1) * n] = high
        w_ref[(2 + part) * n : (3 + part) * n] = (full - high.astype(jnp.float32)).astype(jnp.bfloat16)


def channelize_kernel(plan, taps_ref, flags_ref, v_ref, next_ref, o_ref, w_ref, keep_ref):
    n = plan.n

    @pl.when(pl.program_id(0) == 0)
    def _():
        filter_matrix(plan, taps_ref, w_ref)
        antenna = lax.broadcasted_iota(jnp.int32, (8, plan.rows), 1) // 2
        keep = jnp.zeros((8, plan.rows), jnp.float32)
        for index in range(plan.count):
            keep = jnp.where(antenna == index, flags_ref[index].astype(jnp.float32), keep)
        keep_ref[...] = keep / math.sqrt(plan.chans)

    keep = keep_ref[:1]
    lane = lax.broadcasted_iota(jnp.int32, (plan.rows, plan.next), 1)
    after = next_ref[...].reshape(plan.rows, plan.next)
    after = jnp.where(lane < plan.behind, after.astype(jnp.float32), 0.0).astype(jnp.bfloat16)

    def body(first, last):
        base = first * plan.step * plan.block
        need = plan.step * plan.block + plan.window - plan.block
        if last:
            x = v_ref[:, :, plan.samples - plan.step * plan.block :].reshape(plan.rows, plan.step * plan.block)
            x = jnp.concatenate([x, after[:, : need - plan.step * plan.block]], axis=1)
        else:
            x = v_ref[:, :, pl.ds(base, need)].reshape(plan.rows, need)
        x = jnp.concatenate([x[:, i * plan.block : i * plan.block + plan.window] for i in range(plan.step)], axis=0)
        d = dot(w_ref[...], x, NT)
        d = d[: 2 * n] + d[2 * n :]
        out = []
        for i in range(plan.step):
            at = slice(i * plan.rows, (i + 1) * plan.rows)
            out.append((d[:n, at] - swap_pairs(d[n:, at])) * keep)
        if plan.direct:
            for chan in range(plan.chans):
                at = slice(chan * plan.per, (chan + 1) * plan.per)
                both = jnp.concatenate([piece[at] for piece in out], axis=0)
                o_ref[chan, first * PACK : (first + 1) * PACK, :] = both.astype(jnp.bfloat16)
        else:
            o_ref[first] = jnp.concatenate(out, axis=1).astype(jnp.bfloat16)

    steps = plan.part // PACK
    for first in range(steps):
        body(first, first == steps - 1)


def channelize(voltages, taps, flags, first, parts):
    count, _, length = voltages.shape
    ntaps, chans = taps.shape
    plan = Plan(count, length, ntaps, chans)
    steps = plan.part // PACK
    ratio = plan.samples // plan.next
    if plan.direct:
        shape = (chans, parts * plan.part, plan.rows)
        out_spec = pl.BlockSpec((chans, plan.part, plan.rows), lambda i: (0, i, 0))
    else:
        shape = (parts * steps, plan.n, plan.step * plan.rows)
        out_spec = pl.BlockSpec((steps, plan.n, plan.step * plan.rows), lambda i: (i, 0, 0))
    samples = parts * plan.samples
    out = pl.pallas_call(
        functools.partial(channelize_kernel, plan),
        grid=(parts,),
        in_specs=[
            pl.BlockSpec(memory_space=pltpu.SMEM),
            pl.BlockSpec(memory_space=pltpu.SMEM),
            pl.BlockSpec((count, 2, plan.samples), lambda i: (0, 0, first + i)),
            pl.BlockSpec((count, 2, plan.next), lambda i: (0, 0, (first + i + 1) * ratio)),
        ],
        out_specs=out_spec,
        out_shape=jax.ShapeDtypeStruct(shape, jnp.bfloat16),
        scratch_shapes=[
            pltpu.VMEM((4 * plan.n, plan.window), jnp.bfloat16),
            pltpu.VMEM((8, plan.rows), jnp.float32),
        ],
        cost_estimate=pl.CostEstimate(
            flops=8 * plan.n * plan.window * plan.rows * samples // plan.block,
            bytes_accessed=8 * plan.rows * samples,
            transcendentals=0,
        ),
        name="channelize",
    )(taps, flags, voltages, voltages)
    if not plan.direct:
        out = out.reshape(parts * steps, chans, plan.per, plan.step, plan.rows)
        out = out.transpose(1, 0, 3, 2, 4).reshape(chans, parts * plan.part, plan.rows)
    return out


def steer_kernel(scale_ref, positions_ref, index_ref, o_ref):
    beams = index_ref.shape[1]
    row = lax.broadcasted_iota(jnp.int32, (beams, beams), 0)
    lane = lax.broadcasted_iota(jnp.int32, (beams, beams), 1)

    def column(line):
        return jnp.sum(jnp.where(row == lane, line, 0.0), axis=1, keepdims=True)

    index = index_ref[...]
    east = column((index % grid_side).astype(jnp.float32))
    north = column((index // grid_side).astype(jnp.float32))
    east = (east + 0.5) / grid_side - 0.5
    north = (north + 0.5) / grid_side - 0.5
    ratio = scale_ref[...]
    width = 2 * LANES

    def body(i, carry):
        where = pl.ds(pl.multiple_of(i * width, width), width)
        turns = ratio * (positions_ref[0:1, where] * east + positions_ref[1:2, where] * north)
        turns = turns - jnp.round(turns)
        odd = lax.broadcasted_iota(jnp.int32, turns.shape, 1) % 2
        turns = jnp.where(odd == 1, turns + 0.25, turns)
        turns = turns - jnp.round(turns)
        o_ref[:, where] = cos_turns(turns)
        return carry

    lax.fori_loop(0, positions_ref.shape[1] // width, body, 0)


def cos_turns(t):
    u = 0.25 - jnp.abs(t)
    s = u * u
    acc = jnp.full_like(s, SINE[-1])
    for c in SINE[-2::-1]:
        acc = acc * s + c
    return acc * u


def sin_turns(t):
    return jnp.where(t < 0, -1.0, 1.0) * cos_turns(jnp.abs(t) - 0.25)


SINE = [(-1) ** k * (2.0 * math.pi) ** (2 * k + 1) / math.factorial(2 * k + 1) for k in range(8)]


def steering(channel, positions, beam_index, chans):
    count = positions.shape[1]
    beams = beam_index.shape[0]
    ratio = (1.0 + 0.5 * channel.astype(jnp.float32) / chans).reshape(1, 1)
    return pl.pallas_call(
        steer_kernel,
        out_shape=jax.ShapeDtypeStruct((beams, 2 * count), jnp.float32),
        cost_estimate=pl.CostEstimate(flops=60 * beams * count, bytes_accessed=8 * beams * count, transcendentals=0),
        name="steer",
    )(ratio, jnp.repeat(positions, 2, axis=1), beam_index[None, :])


def solve_kernel(*refs):
    steer_hbm, *x_refs = refs[:-7]
    o_ref, xx_ref, steer_ref, w_ref, low_ref, u_ref, sem = refs[-7:]
    fetch = pltpu.make_async_copy(steer_hbm, steer_ref, sem)
    fetch.start()
    sources, _, width = x_refs[0].shape
    total = sum(x_ref.shape[1] for x_ref in x_refs)
    lanes = sources * width
    count = lanes // 2

    squares = []
    for src in range(sources):
        where = slice(src * width, (src + 1) * width)
        acc = jnp.zeros((8, width), jnp.float32)
        start = 0
        for x_ref in x_refs:
            size = math.gcd(x_ref.shape[1], 64)
            for i in range(0, x_ref.shape[1], size):
                x = x_ref[src, i : i + size, :]
                f = x.astype(jnp.float32)
                at = start + i
                xx_ref[at : at + size, where] = x
                xx_ref[total + at : total + at + size, where] = swap_pairs(f).astype(jnp.bfloat16)
                acc = acc + jnp.sum((f * f).reshape(size // 8, 8, width), axis=0)
            start += x_ref.shape[1]
        squares.append(jnp.sum(acc, axis=0, keepdims=True))
    square = jnp.concatenate(squares, axis=1)
    lane = lax.broadcasted_iota(jnp.int32, square.shape, 1)
    other = jnp.where(lane % 2 == 0, pltpu.roll(square, lanes - 1, 1), pltpu.roll(square, 1, 1))
    diagonal = (square + other) / total
    loading = jnp.sum(square, axis=1, keepdims=True) / (total * count) + 1e-05
    scaling = damping / (diagonal + loading)

    fetch.wait()
    w = scaling * steer_ref[...]
    w_ref[...] = w
    low_ref[...] = w.astype(jnp.bfloat16)
    tile = 512

    def project():
        def body(i, carry):
            at = pl.ds(pl.multiple_of(i * tile, tile), tile)
            u_ref[:, at] = dot(low_ref[...], xx_ref[at, :], NT)
            return carry

        lax.fori_loop(0, 2 * total // tile, body, 0)

    for _ in range(ITERS):
        project()
        u_low = (u_ref[...] / total).astype(jnp.bfloat16)
        for i in range(lanes // tile):
            at = slice(i * tile, (i + 1) * tile)
            image = dot(u_low, xx_ref[:, at], NN)
            w = w_ref[:, at]
            w = w + scaling[:, at] * (steer_ref[:, at] - (image + loading * w))
            w_ref[:, at] = w
            low_ref[:, at] = w.astype(jnp.bfloat16)
    project()

    beam = (u_ref[...] * (1.0 / math.sqrt(count))).astype(jnp.bfloat16).astype(jnp.float32)
    square = beam * beam
    energy = square[:, :total] + square[:, total:]
    high = energy.astype(jnp.bfloat16)
    rest = (energy - high.astype(jnp.float32)).astype(jnp.bfloat16)
    row = lax.broadcasted_iota(jnp.int32, (total, total // group), 0)
    lane = lax.broadcasted_iota(jnp.int32, (total, total // group), 1)
    pick = jnp.where(row // group == lane, 1.0, 0.0).astype(jnp.bfloat16)
    o_ref[...] = (dot(high, pick, NN) + dot(rest, pick, NN)).astype(jnp.bfloat16)


def solve(steer, xs):
    beams, lanes = steer.shape
    total = sum(x.shape[1] for x in xs)
    return pl.pallas_call(
        solve_kernel,
        in_specs=[pl.BlockSpec(memory_space=pl.ANY)] + [pl.BlockSpec(memory_space=pltpu.VMEM)] * len(xs),
        out_specs=pl.BlockSpec(memory_space=pltpu.VMEM),
        out_shape=jax.ShapeDtypeStruct((beams, total // group), jnp.bfloat16),
        scratch_shapes=[
            pltpu.VMEM((2 * total, lanes), jnp.bfloat16),
            pltpu.VMEM((beams, lanes), jnp.float32),
            pltpu.VMEM((beams, lanes), jnp.float32),
            pltpu.VMEM((beams, lanes), jnp.bfloat16),
            pltpu.VMEM((beams, 2 * total), jnp.float32),
            pltpu.SemaphoreType.DMA,
        ],
        compiler_params=pltpu.CompilerParams(vmem_limit_bytes=40 * 2**20),
        cost_estimate=pl.CostEstimate(flops=20 * beams * total * lanes, bytes_accessed=2**22, transcendentals=0),
        name="solve",
    )(steer, *xs)


def local(voltages, taps, flags, positions, beam_index):
    chans = taps.shape[1]
    peers = lax.axis_size("wide")
    per_dev = chans // peers
    first = lax.axis_index("wide") * per_dev
    plan = Plan(voltages.shape[0], voltages.shape[2], *taps.shape)
    parts = plan.total // plan.part
    sizes = [size * parts // sum(CHUNKS) for size in CHUNKS]
    moved = []
    start = 0
    for size in sizes:
        spectra = channelize(voltages, taps, flags, start, size)
        piece = lax.all_to_all(spectra, "wide", split_axis=0, concat_axis=0, tiled=True)
        moved.append(piece.reshape(peers, per_dev, size * plan.part, plan.rows))
        start += size
    spectra, positions, beam_index = lax.optimization_barrier((spectra, positions, beam_index))
    powers = []
    for offset in range(per_dev):
        steer = steering(first + offset, positions, beam_index, chans)
        xs = []
        for piece in moved:
            x = piece[:, offset]
            if plan.rows % LANES:
                x = x.transpose(1, 0, 2).reshape(1, x.shape[1], peers * plan.rows)
            xs.append(x)
        powers.append(solve(steer, xs))
    beams = beam_index.shape[0]
    power = jnp.stack(powers).reshape(per_dev, peers, beams // peers, -1).transpose(1, 0, 2, 3)
    result = lax.all_to_all(power, "wide", split_axis=0, concat_axis=0, tiled=True)
    result = result.reshape(chans, beams // peers, -1)
    return jnp.transpose(result.astype(jnp.float32), (1, 0, 2))


def solution(mesh):
    in_specs = (P(("grp", "wide"), None, None), P(), P(("grp", "wide")), P(), P("grp"))
    out_specs = P(("grp", "wide"), None, None)
    return jax.shard_map(local, mesh=mesh, in_specs=in_specs, out_specs=out_specs, check_vma=False)
```

time: 108 us -> 84.8 us (0.79)
  Pallas kernels: 39 us -> 20.9 us
  local copies, waits for them, and re-layouts: 6.62 us -> 3.83 us
  other arithmetic: 1.8 us -> 0.01 us
    pallas_call x2, Pallas kernels: 33.8 us -> 15.7 us  [the longest x1 9.29 us: solve(): pl.pallas_call(solve_kernel, in_specs=[pl.BlockSpec(memory_space=pl.ANY)]...]
    another operation x4 -> x0, local copies, waits for them, and re-layouts: 2.13 us -> none  [the longest x2 1.36 us: channelize(): wide_taps = jnp.tile(taps, (1, plan.window // chans))]
    unnamed x7 -> x4, local copies, waits for them, and re-layouts: 2.18 us -> 1.59 us
  transfers between devices with their start and end apart: 1 -> 1, of which waited for: 1 -> 1; matrix products, arithmetic and copies ran while one was open for 1% -> 2% of each run, Pallas kernels for 5% -> 6%
where the time goes in v1:
time: 84.8 us; the launch traced here: 84.5 us
  waiting for transfers between devices  34.2 us (40%)
  Pallas kernels  20.9 us (25%)
  blocking collectives  17.9 us (21%)
  starting transfers between devices  7.55 us (9%)
  local copies, waits for them, and re-layouts  3.83 us (5%)
    all_to_all x1, waiting for transfers between devices, local(): lax.all_to_all(spectra, 'wide', split_axis=0, concat_axis=0, tiled=True)  34.2 us
    all_to_all x1, blocking collectives, local(): lax.all_to_all(power, 'wide', split_axis=0, concat_axis=0, tiled=True)  17.9 us
    pallas_call x1, Pallas kernels, solve(): pl.pallas_call(solve_kernel, in_specs=[pl.BlockSpec(memory_space=pl.ANY)]...  9.29 us
    all_to_all x1, starting transfers between devices, local(): lax.all_to_all(spectra, 'wide', split_axis=0, concat_axis=0, tiled=True)  7.55 us
    pallas_call x1, Pallas kernels, channelize(): pl.pallas_call(functools.partial(channelize_kernel, plan), grid=(parts,),...  6.4 us
    pallas_call x1, Pallas kernels, steering(): pl.pallas_call(steer_kernel, out_shape=jax.ShapeDtypeStruct((beams, 2 * c...  5.2 us
  transfers between devices with their start and end apart: 1, of which 1 were waited for; matrix products, arithmetic and copies ran while one was open for 2% of the time, Pallas kernels for 6%

profile of v1, /device:TPU:0, one launch (start us, length us, event | category | flops | bytes accessed | tf_op | source)
XLA Modules:
  0.0 84.5 jit_solution(6675957203150695464)
XLA Ops:
  0.0 6.4 %channelize.1 = bf16[16,512,128]{2,1,0:T(8,128)(2,1)} custom-call(f32[4,16]{1,0:T(4,128)} %taps_ref.1, s32[64]{0:T(128)} %flags_ref.1, bf16[64,2,8240]{2,1,0:T(2,128)(2,1)} %next_ref.1, bf16[64,2,8240]{2,1,0:T(2,128)(2,1)} %next_ref.1), custom_call_target="tpu_custom_call" | custom-call | flops 2147483648 | bytes 8388608 | tf_op jit(solution)/shard_map/channelize/pallas_call | solution.py:148
  6.4 0.0 copy-start.1
  6.4 7.5 %all-to-all-start = ((bf16[16,512,128]{2,1,0:T(8,128)(2,1)}), bf16[16,512,128]{2,1,0:T(8,128)(2,1)S(1)}, u32[]{:S(2)}, u32[]{:S(2)}) async-start(bf16[16,512,128]{2,1,0:T(8,128)(2,1)} %channelize.1), calls=%async_computation | async-start | bytes 4194304 | tf_op jit(solution)/shard_map/all_to_all | solution.py:337
  14.0 0.0 copy-done.1
  14.0 0.3 broadcast_in_dim.6
  14.3 1.2 %reshape.10.positions_ref = f32[2,2048]{1,0:T(2,128)} reshape(f32[2,1024,2]{2,1,0:T(8,128)S(1)} %broadcast_in_dim.6) | data formatting | bytes 32768 | tf_op jit(solution)/shard_map/reshape | solution.py:230
  15.5 5.2 %steer.1.refs_0_ = f32[256,2048]{1,0:T(8,128)} custom-call(f32[1,1]{1,0:T(1,128)} %bitcast.scale_ref, f32[2,2048]{1,0:T(2,128)} %reshape.10.positions_ref, s32[1,256]{1,0:T(1,128)} %bitcast.11), custom_call_target="tpu_custom_call" | custom-call | flops 15728640 | bytes 2097152 | tf_op jit(solution)/shard_map/steer/pallas_call | solution.py:225
  20.7 34.2 %all-to-all-done.refs_1_ = bf16[16,512,128]{2,1,0:T(8,128)(2,1)S(1)} async-done(((bf16[16,512,128]{2,1,0:T(8,128)(2,1)}), bf16[16,512,128]{2,1,0:T(8,128)(2,1)S(1)}, u32[]{:S(2)}, u32[]{:S(2)}) %all-to-all-start) | async-done | bytes 2097184 | tf_op jit(solution)/shard_map/all_to_all | solution.py:337
  54.9 0.0 copy-start
  54.9 1.6 %copy-done = f32[256,2048]{1,0:T(8,128)S(1)} copy-done((f32[256,2048]{1,0:T(8,128)S(1)}, f32[256,2048]{1,0:T(8,128)}, u32[]{:S(2)}) %copy-start) | copy-done | bytes 2097176
  56.5 9.3 %solve.1 = bf16[256,128]{1,0:T(8,128)(2,1)S(1)} custom-call(f32[256,2048]{1,0:T(8,128)S(1)} %copy-done, bf16[16,512,128]{2,1,0:T(8,128)(2,1)S(1)} %all-to-all-done.refs_1_), custom_call_target="tpu_custom_call" | custom-call | flops 5368709120 | bytes 4194304 | tf_op jit(solution)/shard_map/solve/pallas_call | solution.py:306
  65.8 17.9 %all_to_all.10 = bf16[16,1,16,128]{3,2,1,0:T(8,128)(2,1)S(1)} all-to-all(bf16[16,1,16,128]{3,2,1,0:T(8,128)(2,1)S(1)} %bitcast.10), channel_id=1, replica_groups=mesh['grp'=2,'wide'=16] {'wide'}, dimensions={0} | all-to-all | bytes 131072 | tf_op jit(solution)/shard_map/all_to_all | solution.py:353
  83.8 0.7 copy.9
  (1 shorter events, 0.0 us)
Async XLA Ops:
  6.4 7.6 %copy-start.1 = (f32[2,1024]{1,0:T(2,128)S(1)}, f32[2,1024]{1,0:T(2,128)}, u32[]{:S(2)}) copy-start(f32[2,1024]{1,0:T(2,128)} %param.8) | copy-start | bytes 24580
  6.4 48.5 %all-to-all-start = ((bf16[16,512,128]{2,1,0:T(8,128)(2,1)}), bf16[16,512,128]{2,1,0:T(8,128)(2,1)S(1)}, u32[]{:S(2)}, u32[]{:S(2)}) async-start(bf16[16,512,128]{2,1,0:T(8,128)(2,1)} %channelize.1), calls=%async_computation | async-start | bytes 4194304 | tf_op jit(solution)/shard_map/all_to_all | solution.py:337
  54.9 1.6 %copy-start = (f32[256,2048]{1,0:T(8,128)S(1)}, f32[256,2048]{1,0:T(8,128)}, u32[]{:S(2)}) copy-start(f32[256,2048]{1,0:T(8,128)} %steer.1.refs_0_) | copy-start | bytes 6291460
